TPU v7x, 32 devices: a whole 2x2x4 slice. The times are simulated.
32 devices in a mesh: fact: 4 (over z), dim: 8 (over y, x, core).
Axes of the slice: x: 2, y: 2, z: 4, core: 2. Of those that a mesh axis runs over, the one named last changes fastest.
Arguments:
- facts: bfloat16 [4096, 512], P(('fact', 'dim')), may hold values from -6 to 6
- dims: bfloat16 [4096, 512], P(('fact', 'dim')), may hold values from -6 to 6
- tiles: bfloat16 [1024, 128, 128], P(('fact', 'dim')), may hold values from -0.125 to 0.125
- links: int32 [1024, 2], P(('fact', 'dim')), may hold values from 0 to 31, as said below
- link_count: int32 [32], P(('fact', 'dim')), may hold values from 8 to 32, as said below
- block_table: int32 [32], replicated, may hold values from 0 to 2
- w_self: bfloat16 [512, 512], replicated, may hold values from -0.25 to 0.25
- w_tables: bfloat16 [3, 512, 512], replicated, may hold values from -0.25 to 0.25
- cot: bfloat16 [4096, 512], P(('fact', 'dim')), may hold values from -6 to 6
Outputs:
- fact_out: bfloat16 [4096, 512], P(('fact', 'dim'))
- grad_dims: float32 [4096, 512], P(('fact', 'dim'))
- grad_w_self: float32 [512, 512], replicated
- grad_w_tables: float32 [3, 512, 512], replicated
Inputs may be any that keep to these rules, and one draw needn't show every extreme that they name: On device k = f * 8 + d (f, d its fact and dim indices), links[l,0] is a fact block among those of rows f * 128 * 8 to (f + 1) * 128 * 8 - 1, and links[l,1] is a dimension block held by a device with dim index d, i.e. links[l,1] % 8 == d. Slots beyond the device's count hold such indices too and are padding. `link_count`: some device has all 32 slots live and some device exactly 8.
All inputs are finite; a program needn't handle non-finite values.
Results may differ from a plain program's by a relative error of at most 0.017.
Values may be sent and summed in bfloat16 or wider, within the bound.
A program may use at most 64 MiB of HBM per device.

v0:
```python
import functools

import jax
import jax.numpy as jnp
from jax import lax
from jax.experimental import pallas as pl
from jax.experimental.pallas import tpu as pltpu
from jax.sharding import PartitionSpec as P

MESH = pl.DeviceIdType.MESH
BF = jnp.bfloat16
F32 = jnp.float32
CORES = 2
STAGES = 2


def dot(a, b):
    return jnp.dot(a, b, preferred_element_type=F32)


def flip(x):
    return x.astype(F32).T.astype(BF)


def prep_kernel(dims_n, links, count, table, tiles, facts, dims, w_tables, adj, proj, chunks, acc):
    n_fact, n_dim = dims_n
    chips = n_dim // CORES
    block = tiles.shape[1]
    f = lax.axis_index("fact")
    d = lax.axis_index("dim")
    acc[...] = jnp.zeros_like(acc)
    own = table[f * n_dim + d]
    both = dot(dims[...], w_tables[own]).astype(BF)
    cut = proj.shape[2]
    for h in range(proj.shape[0]):
        proj[h] = both[:, h * cut : (h + 1) * cut]

    def add(l, _):
        i = links[0, l] - f * n_dim
        row = lax.rem(i, CORES) * chips + lax.div(i, CORES)
        col = lax.div(links[1, l], n_dim)
        acc[row, col] += tiles[l].astype(F32)
        return 0

    lax.fori_loop(0, count[0], add, 0)
    depth = chunks.shape[1] // 2
    facts_t = flip(facts[...])
    dims_t = flip(dims[...])
    for c in range(chips):
        chunks[c, :depth] = facts_t[c * depth : (c + 1) * depth]
        chunks[c, depth:] = dims_t[c * depth : (c + 1) * depth]
    for i in range(n_dim):
        for j in range(n_fact):
            adj[i * block : (i + 1) * block, j * block : (j + 1) * block] = acc[i, j].astype(BF)


def main_kernel(
    dims_n, table, adj, proj, chunks, facts, cot, w_self, w_tables,
    fact_out, grad_dims, weights,
    panel, adj_t, chunk_all, masked, pre, send1, recv1, mine, send2, recv2, gp, grad,
    send3, recv3, gs, gs_all, w_own, w_send, w_recv,
    a_s, a_r, f_s, f_r, b1_s, b1_r, b2_s, b2_r, c_s, c_r, cp_s, cp_r,
    d_s, d_r, e_s, e_r, w_s, w_r, z_s, z_r, p_s, p_r, q_s, q_r,
):
    n_fact, n_dim = dims_n
    chips = n_dim // CORES
    rows, width = facts.shape
    cut = width // STAGES
    thin = cut // CORES
    depth = chunks.shape[1] // 2
    tables = w_tables.shape[0]
    per = n_fact // (tables + 1)
    part = depth // per
    f = lax.axis_index("fact")
    d = lax.axis_index("dim")
    c = lax.div(d, CORES)
    k = lax.rem(d, CORES)
    o = 1 - k
    mate = c * CORES + o
    scale_f = float(rows * n_fact * n_dim) ** -0.5
    started = []

    def send(src, dst, ss, rs, df, dd):
        copy = pltpu.make_async_remote_copy(
            src_ref=src, dst_ref=dst, send_sem=ss, recv_sem=rs,
            device_id=(df, dd), device_id_type=MESH,
        )
        copy.start()
        started.append(copy)
        return copy

    def blk(i):
        return pl.ds(pl.multiple_of(i * rows, rows), rows)

    def cols(h):
        return slice(h * cut, (h + 1) * cut)

    def up(base, j, n):
        return lax.rem(base + j, n)

    barrier = pltpu.get_barrier_semaphore()
    for j in range(1, n_dim):
        pl.semaphore_signal(barrier, inc=1, device_id=(f, up(d, j, n_dim)), device_id_type=MESH)
    for j in range(1, n_fact):
        pl.semaphore_signal(barrier, inc=1, device_id=(up(f, j, n_fact), d), device_id_type=MESH)
    pl.semaphore_wait(barrier, n_dim + n_fact - 2)

    far = sorted(range(1, n_fact), key=lambda j: abs(2 * j - n_fact))
    near = sorted(range(1, n_fact), key=lambda j: min(j, n_fact - j))
    every = range(STAGES)
    rb = k * chips + c
    copies_a = {}
    for h in every:
        for j in far:
            copies_a[h, j] = send(
                proj.at[h], panel.at[h, blk(f)], a_s.at[h, j], a_r.at[h, j], up(f, j, n_fact), d
            )
    copies_f = {}
    for j in range(1, n_dim):
        to = up(d, j, n_dim)
        copies_f[j] = send(
            chunks.at[lax.div(to, CORES)], chunk_all.at[:, blk(rb)], f_s.at[j], f_r.at[j], f, to
        )
    for h in every:
        panel[h, blk(f), :] = proj[h]
        pre[h] = dot(facts[...], w_self[:, cols(h)])
    chunk_all[:, blk(rb)] = chunks[c]
    for i in range(n_dim):
        adj_t[:, i * rows : (i + 1) * rows] = flip(adj[i * rows : (i + 1) * rows, :])

    group = chips * rows

    def grp(i):
        return pl.ds(pl.multiple_of(i * group, group), group)

    order = list(range(1, chips)) + [0]
    copies_1, copies_2, copies_c, copies_m = {}, {}, {}, {}

    def forward(h):
        for j in far:
            copies_a[h, j].wait_recv()
        send1[h] = dot(adj[grp(o), :], panel[h]).astype(BF)
        for j in order:
            at = blk(up(c, j, chips))
            copies_1[h, j] = send(
                send1.at[h, at], recv1.at[h, at], b1_s.at[h, j], b1_r.at[h, j], f, mate
            )
        mine[h] = dot(adj[grp(k), :], panel[h])

    def pair(h):
        for j in order:
            copies_1[h, j].wait_recv()
            chip = up(c, j, chips)
            total = mine[h, blk(chip), :] + recv1[h, blk(chip), :].astype(F32)
            if j:
                send2[h, j] = total.astype(BF)
                copies_2[h, j] = send(
                    send2.at[h, j], recv2.at[h, j], b2_s.at[h, j], b2_r.at[h, j],
                    f, chip * CORES + k,
                )
            else:
                pre[h] += total

    def activate(h):
        total = pre[h]
        for j in range(1, chips):
            copies_2[h, j].wait_recv()
            total = total + recv2[h, j].astype(F32)
        sig = 1.0 / (1.0 + jnp.exp(-total))
        gp[h, blk(rb), :] = (
            cot[:, cols(h)].astype(F32) * sig * (1.0 + total * (1.0 - sig))
        ).astype(BF)
        src = gp.at[h, blk(rb)]
        for j in range(1, chips):
            copies_c[h, j] = send(
                src, src, c_s.at[h, j], c_r.at[h, j], f, up(c, j, chips) * CORES + k
            )
        copies_m[h, 0] = send(src, src, cp_s.at[h, 0], cp_r.at[h, 0], f, mate)
        fact_out[:, cols(h)] = (total * sig).astype(BF)

    def share(h):
        for j in range(1, chips):
            copies_c[h, j].wait_recv()
            src = gp.at[h, blk(k * chips + up(c, chips - j, chips))]
            copies_m[h, j] = send(src, src, cp_s.at[h, j], cp_r.at[h, j], f, mate)

    def mask():
        for j in range(1, n_dim):
            copies_f[j].wait_recv()
        for i in range(n_dim):
            source = (i % chips) * CORES + i // chips
            name = table[f * n_dim + source]
            lanes = slice(i * rows, (i + 1) * rows)
            values = chunk_all[depth:, lanes].astype(F32)
            for t in range(tables):
                masked[t * depth : (t + 1) * depth, lanes] = (
                    values * (name == t).astype(F32)
                ).astype(BF)

    copies_d, copies_e, copies_w = {}, {}, {}

    def backward(h):
        grad[h] = dot(adj_t[:, grp(k)], gp[h, grp(k), :])
        for j in range(chips):
            copies_m[h, j].wait_recv()
        grad[h] += dot(adj_t[:, grp(o)], gp[h, grp(o), :])
        for j in far:
            to = up(f, j, n_fact)
            send3[h, j] = grad[h, blk(to), :].astype(BF)
            copies_d[h, j] = send(
                send3.at[h, j], recv3.at[h, j], d_s.at[h, j], d_r.at[h, j], to, d
            )

    side = pl.ds(pl.multiple_of(k * thin, thin), thin)

    def own_weight(h):
        w_own[h, :depth, :] = dot(chunk_all[:depth, :], gp[h, :, side]) * scale_f

    def collect(h):
        total = grad[h, blk(f), :]
        for j in near:
            copies_d[h, j].wait_recv()
            total = total + recv3[h, j].astype(F32)
        rounded = total.astype(BF)
        for i in range(CORES):
            gs[h, i] = rounded[:, i * thin : (i + 1) * thin]
        for j in range(1, n_dim):
            to = up(d, j, n_dim)
            copies_e[h, j] = send(
                gs.at[h, lax.rem(to, CORES)], gs_all.at[h, blk(rb)], e_s.at[h, j], e_r.at[h, j],
                f, to,
            )
        gs_all[h, blk(rb), :] = gs[h, k]
        own = table[f * n_dim + d]
        term = lax.dot_general(
            rounded, w_tables[own, :, cols(h)], (((1,), (1,)), ((), ())),
            preferred_element_type=F32,
        )
        if h:
            grad_dims[...] += term
        else:
            grad_dims[...] = term

    def unit(i):
        return pl.ds(pl.multiple_of(i * part, part), part)

    def table_weight(h):
        for j in range(1, n_dim):
            copies_e[h, j].wait_recv()
        w_own[h, depth:, :] = dot(masked[...], gs_all[h]) * scale_f
        for j in far:
            to = up(f, j, n_fact)
            w_send[h, j] = w_own[h, unit(to), :].astype(BF)
            copies_w[h, j] = send(
                w_send.at[h, j], w_recv.at[h, j], w_s.at[h, j], w_r.at[h, j], to, d
            )

    def place(h, ff, cc, kk):
        return (
            lax.div(ff, per),
            pl.ds(pl.multiple_of(cc * depth + lax.rem(ff, per) * part, part), part),
            pl.ds(pl.multiple_of(h * cut + kk * thin, thin), thin),
        )

    def region(h, ff, cc, kk):
        return weights.at[place(h, ff, cc, kk)]

    copies_z, copies_p, copies_q = {}, {}, []

    def spread(h, i):
        src = region(h, up(f, n_fact - i, n_fact), c, k)
        for j in range(1, chips):
            copies_p[h, i, j] = send(
                src, src, p_s.at[h, i, j], p_r.at[h, i, j], f, up(c, j, chips) * CORES + k
            )
        copies_q.append(send(src, src, q_s.at[h, i, 0], q_r.at[h, i, 0], f, mate))

    def finish(h):
        total = w_own[h, unit(f), :]
        for j in near:
            copies_w[h, j].wait_recv()
            total = total + w_recv[h, j].astype(F32)
        weights[place(h, f, c, k)] = total.astype(BF)
        src = region(h, f, c, k)
        for j in far:
            copies_z[h, j] = send(
                src, src, z_s.at[h, j], z_r.at[h, j], up(f, j, n_fact), d
            )
        spread(h, 0)

    def relay(h):
        for i in near:
            copies_z[h, i].wait_recv()
            spread(h, i)

    def hand(h):
        for i in [0] + near:
            for j in range(1, chips):
                copies_p[h, i, j].wait_recv()
                src = region(h, up(f, n_fact - i, n_fact), up(c, chips - j, chips), k)
                copies_q.append(send(src, src, q_s.at[h, i, j], q_r.at[h, i, j], f, mate))

    forward(0)
    pair(0)
    forward(1)
    activate(0)
    pair(1)
    mask()
    share(0)
    activate(1)
    backward(0)
    own_weight(0)
    share(1)
    backward(1)
    own_weight(1)
    collect(0)
    table_weight(0)
    collect(1)
    finish(0)
    table_weight(1)
    relay(0)
    finish(1)
    hand(0)
    relay(1)
    hand(1)
    for copy in copies_q:
        copy.wait_recv()
    for copy in started:
        copy.wait_send()


def post_kernel(cuts, out_in, dims_in, weights, fact_out, grad_dims, w_self, w_tables):
    step = pl.program_id(0)

    @pl.when(step == 0)
    def _():
        fact_out[...] = out_in[...]
        grad_dims[...] = dims_in[...]

    @pl.when(step < cuts)
    def _():
        w_self[...] = weights[0].astype(F32)

    @pl.when(step >= cuts)
    def _():
        w_tables[...] = weights[...].astype(F32)


def body(facts, dims, tiles, links, link_count, block_table, w_self, w_tables, cot):
    n_fact = lax.axis_size("fact")
    n_dim = lax.axis_size("dim")
    chips = n_dim // CORES
    rows, width = facts.shape
    block = tiles.shape[1]
    tables = w_tables.shape[0]
    depth = width // chips
    cut = width // STAGES
    thin = cut // CORES
    part = depth * (tables + 1) // n_fact
    dims_n = (n_fact, n_dim)
    cells = n_fact * n_dim * rows * rows
    panes = (n_fact + n_dim) * rows * width
    grant = min(62 << 20, 4 * cells + 16 * panes + 8 * tables * width * width + (6 << 20))
    small = min(62 << 20, 8 * cells + 4 * tables * width * width + (6 << 20))
    vmem = pl.BlockSpec(memory_space=pltpu.VMEM)
    smem = pl.BlockSpec(memory_space=pltpu.SMEM)
    adj, proj, chunks = pl.pallas_call(
        functools.partial(prep_kernel, dims_n),
        out_shape=(
            jax.ShapeDtypeStruct((n_dim * rows, n_fact * rows), BF),
            jax.ShapeDtypeStruct((STAGES, rows, cut), BF),
            jax.ShapeDtypeStruct((chips, 2 * depth, rows), BF),
        ),
        in_specs=[smem, smem, smem, vmem, vmem, vmem, vmem],
        out_specs=(vmem, vmem, vmem),
        scratch_shapes=[pltpu.VMEM((n_dim, n_fact, block, block), F32)],
        compiler_params=pltpu.CompilerParams(vmem_limit_bytes=small),
        name="prep",
    )(links.T, link_count, block_table, tiles, facts, dims, w_tables)

    def sems(*shape):
        return [pltpu.SemaphoreType.DMA((STAGES, *shape))] * 2

    fact_out, grad_dims, weights = pl.pallas_call(
        functools.partial(main_kernel, dims_n),
        out_shape=(
            jax.ShapeDtypeStruct((rows, width), BF),
            jax.ShapeDtypeStruct((rows, width), F32),
            jax.ShapeDtypeStruct((tables + 1, width, width), BF),
        ),
        in_specs=[smem] + [vmem] * 7,
        out_specs=(vmem, vmem, vmem),
        scratch_shapes=[
            pltpu.VMEM((STAGES, n_fact * rows, cut), BF),
            pltpu.VMEM((n_fact * rows, n_dim * rows), BF),
            pltpu.VMEM((2 * depth, n_dim * rows), BF),
            pltpu.VMEM((tables * depth, n_dim * rows), BF),
            pltpu.VMEM((STAGES, rows, cut), F32),
            pltpu.VMEM((STAGES, chips * rows, cut), BF),
            pltpu.VMEM((STAGES, chips * rows, cut), BF),
            pltpu.VMEM((STAGES, chips * rows, cut), F32),
            pltpu.VMEM((STAGES, chips, rows, cut), BF),
            pltpu.VMEM((STAGES, chips, rows, cut), BF),
            pltpu.VMEM((STAGES, n_dim * rows, cut), BF),
            pltpu.VMEM((STAGES, n_fact * rows, cut), F32),
            pltpu.VMEM((STAGES, n_fact, rows, cut), BF),
            pltpu.VMEM((STAGES, n_fact, rows, cut), BF),
            pltpu.VMEM((STAGES, CORES, rows, thin), BF),
            pltpu.VMEM((STAGES, n_dim * rows, thin), BF),
            pltpu.VMEM((STAGES, (tables + 1) * depth, thin), F32),
            pltpu.VMEM((STAGES, n_fact, part, thin), BF),
            pltpu.VMEM((STAGES, n_fact, part, thin), BF),
            *sems(n_fact),
            *[pltpu.SemaphoreType.DMA((n_dim,))] * 2,
            *sems(chips), *sems(chips), *sems(chips), *sems(chips),
            *sems(n_fact), *sems(n_dim), *sems(n_fact), *sems(n_fact),
            *sems(n_fact, chips), *sems(n_fact, chips),
        ],
        compiler_params=pltpu.CompilerParams(
            collective_id=0, has_side_effects=True, vmem_limit_bytes=grant
        ),
        name="main",
    )(block_table, adj, proj, chunks, facts, cot, w_self, w_tables)
    cuts = CORES
    tall = width // cuts
    whole = pl.BlockSpec((rows, width), lambda i: (0, 0))
    return pl.pallas_call(
        functools.partial(post_kernel, cuts),
        out_shape=(
            jax.ShapeDtypeStruct((rows, width), BF),
            jax.ShapeDtypeStruct((rows, width), F32),
            jax.ShapeDtypeStruct((width, width), F32),
            jax.ShapeDtypeStruct((tables, width, width), F32),
        ),
        grid=((tables + 1) * cuts,),
        in_specs=[
            whole, whole, pl.BlockSpec((1, tall, width), lambda i: (i // cuts, i % cuts, 0))
        ],
        out_specs=(
            whole,
            whole,
            pl.BlockSpec((tall, width), lambda i: (jnp.minimum(i, cuts - 1), 0)),
            pl.BlockSpec(
                (1, tall, width),
                lambda i: (jnp.maximum(i // cuts - 1, 0), jnp.where(i < cuts, 0, i % cuts), 0),
            ),
        ),
        compiler_params=pltpu.CompilerParams(vmem_limit_bytes=12 << 20),
        name="post",
    )(fact_out, grad_dims, weights)


def solution(mesh):
    rows = P(("fact", "dim"), None)
    placed = (
        rows,
        rows,
        P(("fact", "dim"), None, None),
        rows,
        P(("fact", "dim")),
        P(),
        P(),
        P(),
        rows,
    )
    return jax.shard_map(
        body,
        mesh=mesh,
        in_specs=placed,
        out_specs=(rows, rows, P(), P()),
        check_vma=False,
    )
```

profile of v0, /device:TPU:0, one launch (start us, length us, event | category | flops | bytes accessed | tf_op | source)
XLA Modules:
  0.0 81.4 jit_solution(11550076715509505074)
XLA Ops:
  0.6 0.0 copy-start.9
  1.3 0.0 copy-start
  1.3 1.4 %copy-done = bf16[3,512,512]{2,1,0:T(8,128)(2,1)S(1)} copy-done((bf16[3,512,512]{2,1,0:T(8,128)(2,1)S(1)}, bf16[3,512,512]{2,1,0:T(8,128)(2,1)}, u32[]{:S(2)}) %copy-start) | copy-done | bytes 1572888
  2.7 0.0 copy-start.2
  2.7 1.2 %copy-done.2 = bf16[32,128,128]{2,1,0:T(8,128)(2,1)S(1)} copy-done((bf16[32,128,128]{2,1,0:T(8,128)(2,1)S(1)}, bf16[32,128,128]{2,1,0:T(8,128)(2,1)}, u32[]{:S(2)}) %copy-start.2) | copy-done | bytes 1048600
  3.9 0.0 copy-start.3
  3.9 0.9 %copy-done.3 = bf16[128,512]{1,0:T(8,128)(2,1)S(1)} copy-done((bf16[128,512]{1,0:T(8,128)(2,1)S(1)}, bf16[128,512]{1,0:T(8,128)(2,1)}, u32[]{:S(2)}) %copy-start.3) | copy-done | bytes 131096
  4.8 0.0 copy-start.6
  4.8 0.9 %copy-done.6 = bf16[128,512]{1,0:T(8,128)(2,1)S(1)} copy-done((bf16[128,512]{1,0:T(8,128)(2,1)S(1)}, bf16[128,512]{1,0:T(8,128)(2,1)}, u32[]{:S(2)}) %copy-start.6) | copy-done | bytes 131096
  5.7 0.0 copy-start.8
  5.7 0.7 copy-done.8
  6.4 0.0 copy-start.10
  6.4 0.7 copy-done.10
  7.1 0.0 copy-start.1
  7.1 0.0 copy-start.4
  7.1 0.0 copy-start.5
  7.1 0.0 copy-start.7
  7.1 1.3 %prep.1 = (bf16[1024,512]{1,0:T(8,128)(2,1)S(1)}, bf16[2,128,256]{2,1,0:T(8,128)(2,1)S(1)}, bf16[4,256,128]{2,1,0:T(8,128)(2,1)S(1)}) custom-call(s32[2,32]{1,0:T(2,128)S(1)} %bitcast.1, s32[1]{0:T(128)S(6)} %copy.13.count, s32[32]{0:T(128)S(1)} %copy-done.8, bf16[32,128,128]{2,1,0:T(8,128)(2,1)S(1)} %copy-done.2, bf16[128,512]{1,0:T(8,128)(2,1)S(1)} %copy-done.3, ...), custom_call_target="tpu_custom_call" | custom-call | tf_op jit(solution)/shard_map/prep/pallas_call | solution.py:367
  8.4 0.0 copy-done.9
  8.4 0.0 copy-done.1
  8.5 0.0 copy-done.4
  8.5 0.1 copy-done.5
  8.6 0.0 copy-done.7
  8.7 68.8 %main.1 = (bf16[128,512]{1,0:T(8,128)(2,1)S(1)}, f32[128,512]{1,0:T(8,128)S(1)}, bf16[4,512,512]{2,1,0:T(8,128)(2,1)S(1)}) custom-call(s32[32]{0:T(128)S(1)} %copy-done.9, bf16[1024,512]{1,0:T(8,128)(2,1)S(1)} %get-tuple-element.10.adj, bf16[2,128,256]{2,1,0:T(8,128)(2,1)S(1)} %get-tuple-element.11.proj, bf16[4,256,128]{2,1,0:T(8,128)(2,1)S(1)} %get-tuple-element.12.chunks, ...), custom_call_target="tpu_custom_call" | custom-call | tf_op jit(solution)/shard_map/main/pallas_call | solution.py:384
  77.5 3.9 %post.1 = (bf16[128,512]{1,0:T(8,128)(2,1)}, f32[128,512]{1,0:T(8,128)}, f32[512,512]{1,0:T(8,128)}, f32[3,512,512]{2,1,0:T(8,128)}) custom-call(bf16[128,512]{1,0:T(8,128)(2,1)S(1)} %get-tuple-element.13.out_in, f32[128,512]{1,0:T(8,128)S(1)} %get-tuple-element.14.dims_in, bf16[4,512,512]{2,1,0:T(8,128)(2,1)S(1)} %get-tuple-element.15.weights), custom_call_target="tpu_custom_call" | custom-call | tf_op jit(solution)/shard_map/post/pallas_call | solution.py:427
Async XLA Ops:
  0.6 7.8 %copy-start.9 = (s32[32]{0:T(128)S(1)}, s32[32]{0:T(128)}, u32[]{:S(2)}) copy-start(s32[32]{0:T(128)} %table.3) | copy-start | bytes 388
  1.3 1.4 %copy-start = (bf16[3,512,512]{2,1,0:T(8,128)(2,1)S(1)}, bf16[3,512,512]{2,1,0:T(8,128)(2,1)}, u32[]{:S(2)}) copy-start(bf16[3,512,512]{2,1,0:T(8,128)(2,1)} %w_tables.3) | copy-start | bytes 4718596
  2.7 1.2 %copy-start.2 = (bf16[32,128,128]{2,1,0:T(8,128)(2,1)S(1)}, bf16[32,128,128]{2,1,0:T(8,128)(2,1)}, u32[]{:S(2)}) copy-start(bf16[32,128,128]{2,1,0:T(8,128)(2,1)} %tiles.1) | copy-start | bytes 3145732
  3.9 0.9 %copy-start.3 = (bf16[128,512]{1,0:T(8,128)(2,1)S(1)}, bf16[128,512]{1,0:T(8,128)(2,1)}, u32[]{:S(2)}) copy-start(bf16[128,512]{1,0:T(8,128)(2,1)} %facts.3) | copy-start | bytes 393220
  4.8 0.9 %copy-start.6 = (bf16[128,512]{1,0:T(8,128)(2,1)S(1)}, bf16[128,512]{1,0:T(8,128)(2,1)}, u32[]{:S(2)}) copy-start(bf16[128,512]{1,0:T(8,128)(2,1)} %dims.1) | copy-start | bytes 393220
  5.7 0.7 copy-start.8
  6.4 0.7 copy-start.10
  7.1 1.4 %copy-start.1 = (bf16[3,512,512]{2,1,0:T(8,128)(2,1)S(1)}, bf16[3,512,512]{2,1,0:T(8,128)(2,1)}, u32[]{:S(2)}) copy-start(bf16[3,512,512]{2,1,0:T(8,128)(2,1)} %w_tables.3) | copy-start | bytes 4718596
  7.1 1.4 %copy-start.4 = (bf16[128,512]{1,0:T(8,128)(2,1)S(1)}, bf16[128,512]{1,0:T(8,128)(2,1)}, u32[]{:S(2)}) copy-start(bf16[128,512]{1,0:T(8,128)(2,1)} %facts.3) | copy-start | bytes 393220
  7.1 1.5 %copy-start.5 = (bf16[512,512]{1,0:T(8,128)(2,1)S(1)}, bf16[512,512]{1,0:T(8,128)(2,1)}, u32[]{:S(2)}) copy-start(bf16[512,512]{1,0:T(8,128)(2,1)} %w_self.1) | copy-start | bytes 1572868
  7.1 1.6 %copy-start.7 = (bf16[128,512]{1,0:T(8,128)(2,1)S(1)}, bf16[128,512]{1,0:T(8,128)(2,1)}, u32[]{:S(2)}) copy-start(bf16[128,512]{1,0:T(8,128)(2,1)} %cot.1) | copy-start | bytes 393220
where the time goes:
time: 81.7 us; the launch traced here: 81.4 us
  Pallas kernels  74.1 us (91%)
  local copies, waits for them, and re-layouts  5.99 us (7%)
  between operations  1.34 us (2%)
    pallas_call x1, Pallas kernels, body(): pl.pallas_call(functools.partial(main_kernel, dims_n), out_shape=(jax.Sha...  68.8 us
    unnamed x22, local copies, waits for them, and re-layouts  5.99 us
    pallas_call x1, Pallas kernels, body(): pl.pallas_call(functools.partial(post_kernel, cuts), out_shape=(jax.Shape...  3.93 us

commit v1 on v0

v1 whole, which is shorter than its diff:
```python
import functools

import jax
import jax.numpy as jnp
from jax import lax
from jax.experimental import pallas as pl
from jax.experimental.pallas import tpu as pltpu
from jax.sharding import PartitionSpec as P

MESH = pl.DeviceIdType.MESH
BF = jnp.bfloat16
F32 = jnp.float32
CORES = 2
STAGES = 4


def dot(a, b):
    return jnp.dot(a, b, preferred_element_type=F32)


def flip(x):
    return x.astype(F32).T.astype(BF)


def prep_kernel(dims_n, links_h, count_h, table_h, tiles_h, w_tables_h, adj, w_one, links, count, table, tiles, acc, sems):
    n_fact, n_dim = dims_n
    chips = n_dim // CORES
    block = tiles.shape[1]
    f = lax.axis_index("fact")
    d = lax.axis_index("dim")
    small = [
        pltpu.make_async_copy(table_h, table, sems.at[0]),
        pltpu.make_async_copy(links_h, links, sems.at[1]),
        pltpu.make_async_copy(count_h, count, sems.at[2]),
    ]
    load = pltpu.make_async_copy(tiles_h, tiles, sems.at[3])
    for copy in small:
        copy.start()
    load.start()
    acc[...] = jnp.zeros_like(acc)
    small[0].wait()
    own = table[f * n_dim + d]
    weight = pltpu.make_async_copy(w_tables_h.at[own], w_one, sems.at[4])
    weight.start()
    small[1].wait()
    small[2].wait()
    load.wait()

    def add(l, _):
        i = links[0, l] - f * n_dim
        row = lax.rem(i, CORES) * chips + lax.div(i, CORES)
        col = lax.div(links[1, l], n_dim)
        acc[row, col] += tiles[l].astype(F32)
        return 0

    lax.fori_loop(0, count[0], add, 0)
    for i in range(n_dim):
        for j in range(n_fact):
            adj[i * block : (i + 1) * block, j * block : (j + 1) * block] = acc[i, j].astype(BF)
    weight.wait()


def main_kernel(
    dims_n, table, adj, w_one, facts, dims, cot, w_self,
    fact_out, grad_dims, weights,
    proj, chunks, panel, adj_t, chunk_all, masked, pre, send1, recv1, mine, send2, recv2, gp, grad,
    send3, recv3, gs, gs_all, w_own, w_send, w_recv,
    a_s, a_r, f_s, f_r, b1_s, b1_r, b2_s, b2_r, c_s, c_r, m_s, m_r,
    d_s, d_r, e_s, e_r, w_s, w_r, z_s, z_r, p_s, p_r, q_s, q_r,
):
    n_fact, n_dim = dims_n
    chips = n_dim // CORES
    rows, width = facts.shape
    cut = width // STAGES
    tables = weights.shape[1] - 1
    depth = chunks.shape[1] // 2
    per = n_fact // (tables + 1)
    part = depth // per
    f = lax.axis_index("fact")
    d = lax.axis_index("dim")
    c = lax.div(d, CORES)
    k = lax.rem(d, CORES)
    o = 1 - k
    mate = c * CORES + o
    scale_f = float(rows * n_fact * n_dim) ** -0.5
    to_f = [lax.rem(f + j, n_fact) for j in range(n_fact)]
    from_f = [lax.rem(f + n_fact - j, n_fact) for j in range(n_fact)]
    to_c = [lax.rem(c + j, chips) for j in range(chips)]
    from_c = [lax.rem(c + chips - j, chips) for j in range(chips)]
    every = range(STAGES)
    far = sorted(range(1, n_fact), key=lambda j: abs(2 * j - n_fact))
    near = sorted(range(1, n_fact), key=lambda j: min(j, n_fact - j))
    order = list(range(1, chips)) + [0]
    rb = k * chips + c
    group = chips * rows

    def remote(src, dst, ss, rs, df, dd):
        return pltpu.make_async_remote_copy(
            src_ref=src, dst_ref=dst, send_sem=ss, recv_sem=rs,
            device_id=(df, dd), device_id_type=MESH,
        )

    def blk(i):
        return pl.ds(pl.multiple_of(i * rows, rows), rows)

    def grp(i):
        return pl.ds(pl.multiple_of(i * group, group), group)

    def unit(i):
        return pl.ds(pl.multiple_of(i * part, part), part)

    def cols(h):
        return slice(h * cut, (h + 1) * cut)

    def holder(h):
        return h % CORES

    def place(h, ff, cc):
        start = pl.multiple_of(cc * depth + lax.rem(ff, per) * part, part)
        return (h, lax.div(ff, per), pl.ds(start, part))

    def region(h, ff, cc):
        return weights.at[place(h, ff, cc)]

    def copy_a(h, j):
        return remote(proj.at[h], panel.at[h, blk(f)], a_s.at[h, j], a_r.at[h, j], to_f[j], d)

    def copy_f(j):
        to = lax.rem(d + j, n_dim)
        return remote(
            chunks.at[lax.div(to, CORES)], chunk_all.at[:, blk(rb)], f_s.at[j], f_r.at[j], f, to
        )

    def copy_1(h, j):
        at = blk(to_c[j])
        return remote(send1.at[h, at], recv1.at[h, at], b1_s.at[h, j], b1_r.at[h, j], f, mate)

    def copy_2(h, j):
        return remote(
            send2.at[h, j], recv2.at[h, j], b2_s.at[h, j], b2_r.at[h, j], f, to_c[j] * CORES + k
        )

    def copy_c(h, j):
        src = gp.at[h, blk(rb)]
        return remote(src, src, c_s.at[h, j], c_r.at[h, j], f, to_c[j] * CORES + k)

    def copy_m(h, j):
        src = gp.at[h, blk(k * chips + from_c[j])]
        return remote(src, src, m_s.at[h, j], m_r.at[h, j], f, mate)

    def copy_d(h, j):
        return remote(
            send3.at[h, j], recv3.at[h, j], d_s.at[h, j], d_r.at[h, j], to_f[j], d
        )

    def copy_e(h, j, source):
        return remote(
            gs.at[h], gs_all.at[h // CORES, blk(rb)], e_s.at[h, j], e_r.at[h, j, source],
            f, to_c[j] * CORES + holder(h),
        )

    def copy_w(h, j):
        return remote(
            w_send.at[h // CORES, j], w_recv.at[h // CORES, j], w_s.at[h, j], w_r.at[h, j],
            to_f[j], d,
        )

    def copy_z(h, j):
        src = region(h, f, c)
        return remote(src, src, z_s.at[h, j], z_r.at[h, j], to_f[j], d)

    def copy_p(h, i, j):
        src = region(h, from_f[i], c)
        return remote(src, src, p_s.at[h, i, j], p_r.at[h, i, j], f, to_c[j] * CORES + k)

    def copy_q(h, i, j):
        src = region(h, from_f[i], from_c[j])
        return remote(src, src, q_s.at[h, i, j], q_r.at[h, i, j], f, mate)

    barrier = pltpu.get_barrier_semaphore()
    for j in range(1, n_fact):
        pl.semaphore_signal(barrier, inc=1, device_id=(to_f[j], d), device_id_type=MESH)
    for j in range(1, n_dim):
        pl.semaphore_signal(
            barrier, inc=1, device_id=(f, lax.rem(d + j, n_dim)), device_id_type=MESH
        )
    both = dot(dims[...], w_one[...]).astype(BF)
    for h in every:
        proj[h] = both[:, cols(h)]
    pl.semaphore_wait(barrier, n_dim + n_fact - 2)

    for h in every:
        for j in far:
            copy_a(h, j).start()
    facts_t = flip(facts[...])
    dims_t = flip(dims[...])
    for i in range(chips):
        chunks[i, :depth] = facts_t[i * depth : (i + 1) * depth]
        chunks[i, depth:] = dims_t[i * depth : (i + 1) * depth]
    for j in range(1, n_dim):
        copy_f(j).start()
    for h in every:
        panel[h, blk(f), :] = proj[h]
        pre[h] = dot(facts[...], w_self[:, cols(h)])
    chunk_all[:, blk(rb)] = chunks[c]
    for i in range(n_dim):
        adj_t[:, i * rows : (i + 1) * rows] = flip(adj[i * rows : (i + 1) * rows, :])

    def forward(h):
        for j in far:
            copy_a(h, j).wait_recv()
        send1[h] = dot(adj[grp(o), :], panel[h]).astype(BF)
        for j in order:
            copy_1(h, j).start()
        mine[h] = dot(adj[grp(k), :], panel[h])

    def pair(h):
        for j in order:
            copy_1(h, j).wait_recv()
            at = blk(to_c[j])
            total = mine[h, at, :] + recv1[h, at, :].astype(F32)
            if j:
                send2[h, j] = total.astype(BF)
                copy_2(h, j).start()
            else:
                pre[h] += total

    def activate(h):
        total = pre[h]
        for j in range(1, chips):
            copy_2(h, j).wait_recv()
            total = total + recv2[h, j].astype(F32)
        sig = 1.0 / (1.0 + jnp.exp(-total))
        gp[h, blk(rb), :] = (
            cot[:, cols(h)].astype(F32) * sig * (1.0 + total * (1.0 - sig))
        ).astype(BF)
        for j in range(1, chips):
            copy_c(h, j).start()
        copy_m(h, 0).start()
        fact_out[:, cols(h)] = (total * sig).astype(BF)

    def share(h):
        for j in range(1, chips):
            copy_c(h, j).wait_recv()
            copy_m(h, j).start()
        grad[h] = dot(adj_t[:, grp(k)], gp[h, grp(k), :])

    def mask():
        for j in range(1, n_dim):
            copy_f(j).wait_recv()
        for i in range(n_dim):
            source = (i % chips) * CORES + i // chips
            name = table[f * n_dim + source]
            lanes = slice(i * rows, (i + 1) * rows)
            values = chunk_all[depth:, lanes].astype(F32)
            for t in range(tables):
                masked[t * depth : (t + 1) * depth, lanes] = (
                    values * (name == t).astype(F32)
                ).astype(BF)

    def backward(h):
        for j in range(chips):
            copy_m(h, j).wait_recv()
        grad[h] += dot(adj_t[:, grp(o)], gp[h, grp(o), :])
        for j in far:
            send3[h, j] = grad[h, blk(to_f[j]), :].astype(BF)
            copy_d(h, j).start()

        @pl.when(k == holder(h))
        def _():
            w_own[h // CORES, :depth, :] = dot(chunk_all[:depth, :], gp[h]) * scale_f

    def collect(h):
        total = grad[h, blk(f), :]
        for j in near:
            copy_d(h, j).wait_recv()
            total = total + recv3[h, j].astype(F32)
        rounded = total.astype(BF)
        gs[h] = rounded
        for j in range(1, chips):
            copy_e(h, j, k).start()

        @pl.when(k != holder(h))
        def _():
            copy_e(h, 0, 1 - holder(h)).start()

        @pl.when(k == holder(h))
        def _():
            gs_all[h // CORES, blk(rb), :] = gs[h]

        term = lax.dot_general(
            rounded, w_one[:, cols(h)], (((1,), (1,)), ((), ())), preferred_element_type=F32
        )
        if h:
            grad_dims[...] += term
        else:
            grad_dims[...] = term

    def table_weight(h):
        @pl.when(k == holder(h))
        def _():
            for j in range(1, chips):
                for source in range(CORES):
                    copy_e(h, j, source).wait_recv()
            copy_e(h, 0, 1 - holder(h)).wait_recv()
            own = h // CORES
            w_own[own, depth:, :] = dot(masked[...], gs_all[own]) * scale_f
            for j in far:
                w_send[own, j] = w_own[own, unit(to_f[j]), :].astype(BF)
                copy_w(h, j).start()

    def finish(h):
        @pl.when(k == holder(h))
        def _():
            own = h // CORES
            total = w_own[own, unit(f), :]
            for j in near:
                copy_w(h, j).wait_recv()
                total = total + w_recv[own, j].astype(F32)
            weights[place(h, f, c)] = total.astype(BF)
            for j in far:
                copy_z(h, j).start()
            for j in range(1, chips):
                copy_p(h, 0, j).start()
            copy_q(h, 0, 0).start()

    def relay(h):
        @pl.when(k == holder(h))
        def _():
            for i in near:
                copy_z(h, i).wait_recv()
                for j in range(1, chips):
                    copy_p(h, i, j).start()
                copy_q(h, i, 0).start()

    def hand(h):
        @pl.when(k == holder(h))
        def _():
            for i in [0] + near:
                for j in range(1, chips):
                    copy_p(h, i, j).wait_recv()
                    copy_q(h, i, j).start()

    tasks = [
        (0.0, forward), (1.5, pair), (5.2, activate), (8.8, share), (9.9, backward),
        (15.4, collect), (19.1, table_weight), (23.4, finish), (27.4, relay), (32.0, hand),
    ]
    step = 2.5
    plan = [(at + step * h, h, task) for at, task in tasks for h in every]
    plan.append((6.0, 0, lambda h: mask()))
    for _, h, task in sorted(plan, key=lambda item: item[:2]):
        task(h)

    for h in every:
        @pl.when(k != holder(h))
        def _():
            for i in range(n_fact):
                for j in range(chips):
                    copy_q(h, i, j).wait_recv()
            copy_e(h, 0, 1 - holder(h)).wait_send()

        @pl.when(k == holder(h))
        def _():
            for j in far:
                copy_w(h, j).wait_send()
                copy_z(h, j).wait_send()
            for i in range(n_fact):
                for j in range(chips):
                    if j:
                        copy_p(h, i, j).wait_send()
                    copy_q(h, i, j).wait_send()

        for j in far:
            copy_a(h, j).wait_send()
            copy_d(h, j).wait_send()
        for j in range(chips):
            copy_1(h, j).wait_send()
            copy_m(h, j).wait_send()
            if j:
                copy_2(h, j).wait_send()
                copy_c(h, j).wait_send()
                copy_e(h, j, k).wait_send()
    for j in range(1, n_dim):
        copy_f(j).wait_send()


def post_kernel(out_in, dims_in, weights, fact_out, grad_dims, w_self, w_tables, wide, sems):
    stages, tables, _, cut = weights.shape
    started = [
        pltpu.make_async_copy(out_in, fact_out, sems.at[tables]),
        pltpu.make_async_copy(dims_in, grad_dims, sems.at[tables + 1]),
    ]
    for copy in started:
        copy.start()
    for t in range(tables):
        for h in range(stages):
            wide[t, :, h * cut : (h + 1) * cut] = weights[h, t].astype(F32)
        copy = pltpu.make_async_copy(
            wide.at[t], w_tables.at[t - 1] if t else w_self, sems.at[t]
        )
        copy.start()
        started.append(copy)
    for copy in started:
        copy.wait()


def body(facts, dims, tiles, links, link_count, block_table, w_self, w_tables, cot):
    n_fact = lax.axis_size("fact")
    n_dim = lax.axis_size("dim")
    chips = n_dim // CORES
    rows, width = facts.shape
    block = tiles.shape[1]
    tables = w_tables.shape[0]
    depth = width // chips
    cut = width // STAGES
    part = depth * (tables + 1) // n_fact
    dims_n = (n_fact, n_dim)
    cells = n_fact * n_dim * rows * rows
    panes = (n_fact + n_dim) * rows * width
    grant = min(62 << 20, 4 * cells + 16 * panes + 8 * tables * width * width + (6 << 20))
    small = min(62 << 20, 8 * cells + 4 * width * width + 2 * tiles.size + (4 << 20))
    vmem = pl.BlockSpec(memory_space=pltpu.VMEM)
    smem = pl.BlockSpec(memory_space=pltpu.SMEM)
    anywhere = pl.BlockSpec(memory_space=pl.ANY)
    adj, w_one = pl.pallas_call(
        functools.partial(prep_kernel, dims_n),
        out_shape=(
            jax.ShapeDtypeStruct((n_dim * rows, n_fact * rows), BF),
            jax.ShapeDtypeStruct((width, width), BF),
        ),
        in_specs=[anywhere] * 5,
        out_specs=(vmem, vmem),
        scratch_shapes=[
            pltpu.SMEM(links.shape[::-1], jnp.int32),
            pltpu.SMEM(link_count.shape, jnp.int32),
            pltpu.SMEM(block_table.shape, jnp.int32),
            pltpu.VMEM(tiles.shape, BF),
            pltpu.VMEM((n_dim, n_fact, block, block), F32),
            pltpu.SemaphoreType.DMA((5,)),
        ],
        compiler_params=pltpu.CompilerParams(vmem_limit_bytes=small),
        name="prep",
    )(links.T, link_count, block_table, tiles, w_tables)

    def sems(*shape):
        return [pltpu.SemaphoreType.DMA((STAGES, *shape))] * 2

    held = STAGES // CORES
    fact_out, grad_dims, weights = pl.pallas_call(
        functools.partial(main_kernel, dims_n),
        out_shape=(
            jax.ShapeDtypeStruct((rows, width), BF),
            jax.ShapeDtypeStruct((rows, width), F32),
            jax.ShapeDtypeStruct((STAGES, tables + 1, width, cut), BF),
        ),
        in_specs=[smem] + [vmem] * 6,
        out_specs=(vmem, vmem, vmem),
        scratch_shapes=[
            pltpu.VMEM((STAGES, rows, cut), BF),
            pltpu.VMEM((chips, 2 * depth, rows), BF),
            pltpu.VMEM((STAGES, n_fact * rows, cut), BF),
            pltpu.VMEM((n_fact * rows, n_dim * rows), BF),
            pltpu.VMEM((2 * depth, n_dim * rows), BF),
            pltpu.VMEM((tables * depth, n_dim * rows), BF),
            pltpu.VMEM((STAGES, rows, cut), F32),
            pltpu.VMEM((STAGES, chips * rows, cut), BF),
            pltpu.VMEM((STAGES, chips * rows, cut), BF),
            pltpu.VMEM((STAGES, chips * rows, cut), F32),
            pltpu.VMEM((STAGES, chips, rows, cut), BF),
            pltpu.VMEM((STAGES, chips, rows, cut), BF),
            pltpu.VMEM((STAGES, n_dim * rows, cut), BF),
            pltpu.VMEM((STAGES, n_fact * rows, cut), F32),
            pltpu.VMEM((STAGES, n_fact, rows, cut), BF),
            pltpu.VMEM((STAGES, n_fact, rows, cut), BF),
            pltpu.VMEM((STAGES, rows, cut), BF),
            pltpu.VMEM((held, n_dim * rows, cut), BF),
            pltpu.VMEM((held, (tables + 1) * depth, cut), F32),
            pltpu.VMEM((held, n_fact, part, cut), BF),
            pltpu.VMEM((held, n_fact, part, cut), BF),
            *sems(n_fact),
            *[pltpu.SemaphoreType.DMA((n_dim,))] * 2,
            *sems(chips), *sems(chips), *sems(chips), *sems(chips),
            *sems(n_fact),
            pltpu.SemaphoreType.DMA((STAGES, chips)),
            pltpu.SemaphoreType.DMA((STAGES, chips, CORES)),
            *sems(n_fact), *sems(n_fact),
            *sems(n_fact, chips), *sems(n_fact, chips),
        ],
        compiler_params=pltpu.CompilerParams(
            collective_id=0, has_side_effects=True, vmem_limit_bytes=grant
        ),
        name="main",
    )(block_table, adj, w_one, facts, dims, cot, w_self)
    return pl.pallas_call(
        post_kernel,
        out_shape=(
            jax.ShapeDtypeStruct((rows, width), BF),
            jax.ShapeDtypeStruct((rows, width), F32),
            jax.ShapeDtypeStruct((width, width), F32),
            jax.ShapeDtypeStruct((tables, width, width), F32),
        ),
        in_specs=[vmem] * 3,
        out_specs=(anywhere,) * 4,
        scratch_shapes=[
            pltpu.VMEM((tables + 1, width, width), F32),
            pltpu.SemaphoreType.DMA((tables + 3,)),
        ],
        compiler_params=pltpu.CompilerParams(vmem_limit_bytes=12 << 20),
        name="post",
    )(fact_out, grad_dims, weights)


def solution(mesh):
    rows = P(("fact", "dim"), None)
    placed = (
        rows,
        rows,
        P(("fact", "dim"), None, None),
        rows,
        P(("fact", "dim")),
        P(),
        P(),
        P(),
        rows,
    )
    return jax.shard_map(
        body,
        mesh=mesh,
        in_specs=placed,
        out_specs=(rows, rows, P(), P()),
        check_vma=False,
    )
```

time: 81.7 us -> 72.8 us (0.89)
  Pallas kernels: 74.1 us -> 67.7 us
  local copies, waits for them, and re-layouts: 5.99 us -> 3.98 us
    pallas_call x1, Pallas kernels: 68.8 us -> 64.2 us  [body(): pl.pallas_call(functools.partial(main_kernel, dims_n), out_shape=(jax.Sha...]
    unnamed x22 -> x18, local copies, waits for them, and re-layouts: 5.99 us -> 3.98 us
    pallas_call x1, Pallas kernels: 3.93 us -> 2.2 us  [body(): pl.pallas_call(post_kernel, out_shape=(jax.ShapeDtypeStruct((rows, width)...]
where the time goes in v1:
time: 72.8 us; the launch traced here: 73.1 us
  Pallas kernels  67.7 us (93%)
  local copies, waits for them, and re-layouts  3.98 us (5%)
  between operations  1.37 us (2%)
    pallas_call x1, Pallas kernels, body(): pl.pallas_call(functools.partial(main_kernel, dims_n), out_shape=(jax.Sha...  64.2 us
    unnamed x18, local copies, waits for them, and re-layouts  3.98 us
    pallas_call x1, Pallas kernels, body(): pl.pallas_call(post_kernel, out_shape=(jax.ShapeDtypeStruct((rows, width)...  2.2 us

profile of v1, /device:TPU:0, one launch (start us, length us, event | category | flops | bytes accessed | tf_op | source)
XLA Modules:
  0.0 73.1 jit_solution(1324376833748706558)
XLA Ops:
  0.6 0.0 copy-start.7
  1.3 0.0 copy-start
  1.3 1.4 %copy-done = bf16[3,512,512]{2,1,0:T(8,128)(2,1)S(1)} copy-done((bf16[3,512,512]{2,1,0:T(8,128)(2,1)S(1)}, bf16[3,512,512]{2,1,0:T(8,128)(2,1)}, u32[]{:S(2)}) %copy-start) | copy-done | bytes 1572888
  2.7 0.0 copy-start.1
  2.7 1.2 %copy-done.1 = bf16[32,128,128]{2,1,0:T(8,128)(2,1)S(1)} copy-done((bf16[32,128,128]{2,1,0:T(8,128)(2,1)S(1)}, bf16[32,128,128]{2,1,0:T(8,128)(2,1)}, u32[]{:S(2)}) %copy-start.1) | copy-done | bytes 1048600
  3.9 0.0 copy-start.6
  3.9 0.7 copy-done.6
  4.6 0.0 copy-start.8
  4.6 0.7 copy-done.8
  5.3 0.0 copy-start.2
  5.3 0.0 copy-start.3
  5.3 0.0 copy-start.4
  5.3 0.0 copy-start.5
  5.3 1.3 %prep.1 = (bf16[1024,512]{1,0:T(8,128)(2,1)S(1)}, bf16[512,512]{1,0:T(8,128)(2,1)S(1)}) custom-call(s32[2,32]{1,0:T(2,128)S(1)} %bitcast.1, s32[1]{0:T(128)S(6)} %copy.13.count_h, s32[32]{0:T(128)S(1)} %copy-done.6, bf16[32,128,128]{2,1,0:T(8,128)(2,1)S(1)} %copy-done.1, bf16[3,512,512]{2,1,0:T(8,128)(2,1)S(1)} %copy-done), custom_call_target="tpu_custom_call" | custom-call | tf_op jit(solution)/shard_map/prep/pallas_call | solution.py:425
  6.6 0.0 copy-done.7
  6.6 0.0 copy-done.2
  6.6 0.0 copy-done.3
  6.7 0.0 copy-done.4
  6.7 0.0 copy-done.5
  6.7 64.2 %main.1 = (bf16[128,512]{1,0:T(8,128)(2,1)S(1)}, f32[128,512]{1,0:T(8,128)S(1)}, bf16[4,4,512,128]{3,2,1,0:T(8,128)(2,1)S(1)}) custom-call(s32[32]{0:T(128)S(1)} %copy-done.7, bf16[1024,512]{1,0:T(8,128)(2,1)S(1)} %get-tuple-element.9.adj, bf16[512,512]{1,0:T(8,128)(2,1)S(1)} %get-tuple-element.10.w_one, bf16[128,512]{1,0:T(8,128)(2,1)S(1)} %copy-done.3, ...), custom_call_target="tpu_custom_call" | custom-call | tf_op jit(solution)/shard_map/main/pallas_call | solution.py:449
  70.9 2.2 %post.1 = (bf16[128,512]{1,0:T(8,128)(2,1)}, f32[128,512]{1,0:T(8,128)}, f32[512,512]{1,0:T(8,128)}, f32[3,512,512]{2,1,0:T(8,128)}) custom-call(bf16[128,512]{1,0:T(8,128)(2,1)S(1)} %get-tuple-element.11.out_in, f32[128,512]{1,0:T(8,128)S(1)} %get-tuple-element.12.dims_in, bf16[4,4,512,128]{3,2,1,0:T(8,128)(2,1)S(1)} %get-tuple-element.13.weights), custom_call_target="tpu_custom_call" | custom-call | tf_op jit(solution)/shard_map/post/pallas_call | solution.py:494
Async XLA Ops:
  0.6 6.0 %copy-start.7 = (s32[32]{0:T(128)S(1)}, s32[32]{0:T(128)}, u32[]{:S(2)}) copy-start(s32[32]{0:T(128)} %table.1) | copy-start | bytes 388
  1.3 1.4 %copy-start = (bf16[3,512,512]{2,1,0:T(8,128)(2,1)S(1)}, bf16[3,512,512]{2,1,0:T(8,128)(2,1)}, u32[]{:S(2)}) copy-start(bf16[3,512,512]{2,1,0:T(8,128)(2,1)} %w_tables_h.1) | copy-start | bytes 4718596
  2.7 1.2 %copy-start.1 = (bf16[32,128,128]{2,1,0:T(8,128)(2,1)S(1)}, bf16[32,128,128]{2,1,0:T(8,128)(2,1)}, u32[]{:S(2)}) copy-start(bf16[32,128,128]{2,1,0:T(8,128)(2,1)} %tiles_h.1) | copy-start | bytes 3145732
  3.9 0.7 copy-start.6
  4.6 0.7 copy-start.8
  5.3 1.4 %copy-start.2 = (bf16[512,512]{1,0:T(8,128)(2,1)S(1)}, bf16[512,512]{1,0:T(8,128)(2,1)}, u32[]{:S(2)}) copy-start(bf16[512,512]{1,0:T(8,128)(2,1)} %w_self.1) | copy-start | bytes 1572868
  5.3 1.4 %copy-start.3 = (bf16[128,512]{1,0:T(8,128)(2,1)S(1)}, bf16[128,512]{1,0:T(8,128)(2,1)}, u32[]{:S(2)}) copy-start(bf16[128,512]{1,0:T(8,128)(2,1)} %facts.1) | copy-start | bytes 393220
  5.3 1.4 %copy-start.4 = (bf16[128,512]{1,0:T(8,128)(2,1)S(1)}, bf16[128,512]{1,0:T(8,128)(2,1)}, u32[]{:S(2)}) copy-start(bf16[128,512]{1,0:T(8,128)(2,1)} %dims.1) | copy-start | bytes 393220
  5.3 1.4 %copy-start.5 = (bf16[128,512]{1,0:T(8,128)(2,1)S(1)}, bf16[128,512]{1,0:T(8,128)(2,1)}, u32[]{:S(2)}) copy-start(bf16[128,512]{1,0:T(8,128)(2,1)} %cot.1) | copy-start | bytes 393220

commit v2 on v1

--- a/solution.py
+++ b/solution.py
@@ -22,7 +22,7 @@
     return x.astype(F32).T.astype(BF)
 
 
-def prep_kernel(dims_n, links_h, count_h, table_h, tiles_h, w_tables_h, adj, w_one, links, count, table, tiles, acc, sems):
+def prep_kernel(dims_n, links_h, count, table_h, tiles_h, w_tables_h, adj, w_one, links, table, tiles, acc, sems):
     n_fact, n_dim = dims_n
     chips = n_dim // CORES
     block = tiles.shape[1]
@@ -31,19 +31,17 @@
     small = [
         pltpu.make_async_copy(table_h, table, sems.at[0]),
         pltpu.make_async_copy(links_h, links, sems.at[1]),
-        pltpu.make_async_copy(count_h, count, sems.at[2]),
     ]
-    load = pltpu.make_async_copy(tiles_h, tiles, sems.at[3])
+    load = pltpu.make_async_copy(tiles_h, tiles, sems.at[2])
     for copy in small:
         copy.start()
     load.start()
     acc[...] = jnp.zeros_like(acc)
     small[0].wait()
     own = table[f * n_dim + d]
-    weight = pltpu.make_async_copy(w_tables_h.at[own], w_one, sems.at[4])
+    weight = pltpu.make_async_copy(w_tables_h.at[own], w_one, sems.at[3])
     weight.start()
     small[1].wait()
-    small[2].wait()
     load.wait()
 
     def add(l, _):
@@ -65,8 +63,7 @@
     fact_out, grad_dims, weights,
     proj, chunks, panel, adj_t, chunk_all, masked, pre, send1, recv1, mine, send2, recv2, gp, grad,
     send3, recv3, gs, gs_all, w_own, w_send, w_recv,
-    a_s, a_r, f_s, f_r, b1_s, b1_r, b2_s, b2_r, c_s, c_r, m_s, m_r,
-    d_s, d_r, e_s, e_r, w_s, w_r, z_s, z_r, p_s, p_r, q_s, q_r,
+    sent, a_r, f_r, b1_r, b2_r, c_r, m_r, d_r, e_r, w_r, z_r, p_r, q_r,
 ):
     n_fact, n_dim = dims_n
     chips = n_dim // CORES
@@ -100,6 +97,9 @@
             device_id=(df, dd), device_id_type=MESH,
         )
 
+    def arrive(ref, sem):
+        pltpu.make_async_copy(ref, ref, sem).wait()
+
     def blk(i):
         return pl.ds(pl.multiple_of(i * rows, rows), rows)
 
@@ -123,59 +123,59 @@
         return weights.at[place(h, ff, cc)]
 
     def copy_a(h, j):
-        return remote(proj.at[h], panel.at[h, blk(f)], a_s.at[h, j], a_r.at[h, j], to_f[j], d)
+        return remote(proj.at[h], panel.at[h, blk(f)], sent.at[0], a_r.at[h], to_f[j], d)
 
     def copy_f(j):
         to = lax.rem(d + j, n_dim)
         return remote(
-            chunks.at[lax.div(to, CORES)], chunk_all.at[:, blk(rb)], f_s.at[j], f_r.at[j], f, to
+            chunks.at[lax.div(to, CORES)], chunk_all.at[:, blk(rb)], sent.at[1], f_r.at[0], f, to
         )
 
     def copy_1(h, j):
         at = blk(to_c[j])
-        return remote(send1.at[h, at], recv1.at[h, at], b1_s.at[h, j], b1_r.at[h, j], f, mate)
+        return remote(send1.at[h, at], recv1.at[h, at], sent.at[2], b1_r.at[h], f, mate)
 
     def copy_2(h, j):
         return remote(
-            send2.at[h, j], recv2.at[h, j], b2_s.at[h, j], b2_r.at[h, j], f, to_c[j] * CORES + k
+            send2.at[h, j], recv2.at[h, j], sent.at[3], b2_r.at[h], f, to_c[j] * CORES + k
         )
 
     def copy_c(h, j):
         src = gp.at[h, blk(rb)]
-        return remote(src, src, c_s.at[h, j], c_r.at[h, j], f, to_c[j] * CORES + k)
+        return remote(src, src, sent.at[4], c_r.at[h], f, to_c[j] * CORES + k)
 
     def copy_m(h, j):
         src = gp.at[h, blk(k * chips + from_c[j])]
-        return remote(src, src, m_s.at[h, j], m_r.at[h, j], f, mate)
+        return remote(src, src, sent.at[5], m_r.at[h], f, mate)
 
     def copy_d(h, j):
         return remote(
-            send3.at[h, j], recv3.at[h, j], d_s.at[h, j], d_r.at[h, j], to_f[j], d
-        )
-
-    def copy_e(h, j, source):
+            send3.at[h, j], recv3.at[h, j], sent.at[6], d_r.at[h], to_f[j], d
+        )
+
+    def copy_e(h, j):
         return remote(
-            gs.at[h], gs_all.at[h // CORES, blk(rb)], e_s.at[h, j], e_r.at[h, j, source],
+            gs.at[h], gs_all.at[h // CORES, blk(rb)], sent.at[7], e_r.at[h],
             f, to_c[j] * CORES + holder(h),
         )
 
     def copy_w(h, j):
         return remote(
-            w_send.at[h // CORES, j], w_recv.at[h // CORES, j], w_s.at[h, j], w_r.at[h, j],
+            w_send.at[h // CORES, j], w_recv.at[h // CORES, j], sent.at[8], w_r.at[h],
             to_f[j], d,
         )
 
     def copy_z(h, j):
         src = region(h, f, c)
-        return remote(src, src, z_s.at[h, j], z_r.at[h, j], to_f[j], d)
+        return remote(src, src, sent.at[9], z_r.at[h, j], to_f[j], d)
 
     def copy_p(h, i, j):
         src = region(h, from_f[i], c)
-        return remote(src, src, p_s.at[h, i, j], p_r.at[h, i, j], f, to_c[j] * CORES + k)
+        return remote(src, src, sent.at[10], p_r.at[h, i], f, to_c[j] * CORES + k)
 
     def copy_q(h, i, j):
         src = region(h, from_f[i], from_c[j])
-        return remote(src, src, q_s.at[h, i, j], q_r.at[h, i, j], f, mate)
+        return remote(src, src, sent.at[11], q_r.at[h], f, mate)
 
     barrier = pltpu.get_barrier_semaphore()
     for j in range(1, n_fact):
@@ -207,16 +207,15 @@
         adj_t[:, i * rows : (i + 1) * rows] = flip(adj[i * rows : (i + 1) * rows, :])
 
     def forward(h):
-        for j in far:
-            copy_a(h, j).wait_recv()
+        arrive(panel.at[h, pl.ds(rows, (n_fact - 1) * rows)], a_r.at[h])
         send1[h] = dot(adj[grp(o), :], panel[h]).astype(BF)
         for j in order:
             copy_1(h, j).start()
         mine[h] = dot(adj[grp(k), :], panel[h])
 
     def pair(h):
+        arrive(recv1.at[h], b1_r.at[h])
         for j in order:
-            copy_1(h, j).wait_recv()
             at = blk(to_c[j])
             total = mine[h, at, :] + recv1[h, at, :].astype(F32)
             if j:
@@ -227,8 +226,8 @@
 
     def activate(h):
         total = pre[h]
+        arrive(recv2.at[h, pl.ds(1, chips - 1)], b2_r.at[h])
         for j in range(1, chips):
-            copy_2(h, j).wait_recv()
             total = total + recv2[h, j].astype(F32)
         sig = 1.0 / (1.0 + jnp.exp(-total))
         gp[h, blk(rb), :] = (
@@ -240,14 +239,13 @@
         fact_out[:, cols(h)] = (total * sig).astype(BF)
 
     def share(h):
+        arrive(recv2.at[h, pl.ds(1, chips - 1)], c_r.at[h])
         for j in range(1, chips):
-            copy_c(h, j).wait_recv()
             copy_m(h, j).start()
         grad[h] = dot(adj_t[:, grp(k)], gp[h, grp(k), :])
 
     def mask():
-        for j in range(1, n_dim):
-            copy_f(j).wait_recv()
+        arrive(chunk_all.at[:, pl.ds(rows, (n_dim - 1) * rows)], f_r.at[0])
         for i in range(n_dim):
             source = (i % chips) * CORES + i // chips
             name = table[f * n_dim + source]
@@ -259,8 +257,7 @@
                 ).astype(BF)
 
     def backward(h):
-        for j in range(chips):
-            copy_m(h, j).wait_recv()
+        arrive(gp.at[h, pl.ds(0, group)], m_r.at[h])
         grad[h] += dot(adj_t[:, grp(o)], gp[h, grp(o), :])
         for j in far:
             send3[h, j] = grad[h, blk(to_f[j]), :].astype(BF)
@@ -272,17 +269,17 @@
 
     def collect(h):
         total = grad[h, blk(f), :]
+        arrive(recv3.at[h, pl.ds(1, n_fact - 1)], d_r.at[h])
         for j in near:
-            copy_d(h, j).wait_recv()
             total = total + recv3[h, j].astype(F32)
         rounded = total.astype(BF)
         gs[h] = rounded
         for j in range(1, chips):
-            copy_e(h, j, k).start()
+            copy_e(h, j).start()
 
         @pl.when(k != holder(h))
         def _():
-            copy_e(h, 0, 1 - holder(h)).start()
+            copy_e(h, 0).start()
 
         @pl.when(k == holder(h))
         def _():
@@ -299,11 +296,8 @@
     def table_weight(h):
         @pl.when(k == holder(h))
         def _():
-            for j in range(1, chips):
-                for source in range(CORES):
-                    copy_e(h, j, source).wait_recv()
-            copy_e(h, 0, 1 - holder(h)).wait_recv()
             own = h // CORES
+            arrive(gs_all.at[own, pl.ds(rows, (n_dim - 1) * rows)], e_r.at[h])
             w_own[own, depth:, :] = dot(masked[...], gs_all[own]) * scale_f
             for j in far:
                 w_send[own, j] = w_own[own, unit(to_f[j]), :].astype(BF)
@@ -314,8 +308,8 @@
         def _():
             own = h // CORES
             total = w_own[own, unit(f), :]
+            arrive(w_recv.at[own, pl.ds(1, n_fact - 1)], w_r.at[h])
             for j in near:
-                copy_w(h, j).wait_recv()
                 total = total + w_recv[own, j].astype(F32)
             weights[place(h, f, c)] = total.astype(BF)
             for j in far:
@@ -328,7 +322,7 @@
         @pl.when(k == holder(h))
         def _():
             for i in near:
-                copy_z(h, i).wait_recv()
+                arrive(region(h, f, c), z_r.at[h, i])
                 for j in range(1, chips):
                     copy_p(h, i, j).start()
                 copy_q(h, i, 0).start()
@@ -337,8 +331,8 @@
         @pl.when(k == holder(h))
         def _():
             for i in [0] + near:
+                arrive(weights.at[h, 0, pl.ds(0, (chips - 1) * part)], p_r.at[h, i])
                 for j in range(1, chips):
-                    copy_p(h, i, j).wait_recv()
                     copy_q(h, i, j).start()
 
     tasks = [
@@ -354,34 +348,24 @@
     for h in every:
         @pl.when(k != holder(h))
         def _():
-            for i in range(n_fact):
-                for j in range(chips):
-                    copy_q(h, i, j).wait_recv()
-            copy_e(h, 0, 1 - holder(h)).wait_send()
-
-        @pl.when(k == holder(h))
-        def _():
-            for j in far:
-                copy_w(h, j).wait_send()
-                copy_z(h, j).wait_send()
-            for i in range(n_fact):
-                for j in range(chips):
-                    if j:
-                        copy_p(h, i, j).wait_send()
-                    copy_q(h, i, j).wait_send()
-
-        for j in far:
-            copy_a(h, j).wait_send()
-            copy_d(h, j).wait_send()
-        for j in range(chips):
-            copy_1(h, j).wait_send()
-            copy_m(h, j).wait_send()
-            if j:
-                copy_2(h, j).wait_send()
-                copy_c(h, j).wait_send()
-                copy_e(h, j, k).wait_send()
-    for j in range(1, n_dim):
-        copy_f(j).wait_send()
+            arrive(weights.at[h], q_r.at[h])
+
+    held = STAGES // CORES
+    for i, ref in enumerate((
+        panel.at[:, pl.ds(rows, (n_fact - 1) * rows)],
+        chunk_all.at[:, pl.ds(rows, (n_dim - 1) * rows)],
+        send1,
+        send2.at[:, pl.ds(1, chips - 1)],
+        send2.at[:, pl.ds(1, chips - 1)],
+        send1,
+        send3.at[:, pl.ds(1, n_fact - 1)],
+        gs_all.at[:, pl.ds(rows, (n_dim - 1) * rows)],
+        w_send.at[:, pl.ds(1, n_fact - 1)],
+        w_send.at[:, pl.ds(1, n_fact - 1)],
+        weights.at[pl.ds(0, held), :, pl.ds(0, width - depth)],
+        weights.at[pl.ds(0, held)],
+    )):
+        arrive(ref, sent.at[i])
 
 
 def post_kernel(out_in, dims_in, weights, fact_out, grad_dims, w_self, w_tables, wide, sems):
@@ -422,28 +406,32 @@
     vmem = pl.BlockSpec(memory_space=pltpu.VMEM)
     smem = pl.BlockSpec(memory_space=pltpu.SMEM)
     anywhere = pl.BlockSpec(memory_space=pl.ANY)
+    hbm = pl.BlockSpec(memory_space=pltpu.HBM)
+
+    def stay(x):
+        return pltpu.with_memory_space_constraint(x, pltpu.HBM)
+
     adj, w_one = pl.pallas_call(
         functools.partial(prep_kernel, dims_n),
         out_shape=(
             jax.ShapeDtypeStruct((n_dim * rows, n_fact * rows), BF),
             jax.ShapeDtypeStruct((width, width), BF),
         ),
-        in_specs=[anywhere] * 5,
+        in_specs=[hbm, smem, hbm, hbm, hbm],
         out_specs=(vmem, vmem),
         scratch_shapes=[
             pltpu.SMEM(links.shape[::-1], jnp.int32),
-            pltpu.SMEM(link_count.shape, jnp.int32),
             pltpu.SMEM(block_table.shape, jnp.int32),
             pltpu.VMEM(tiles.shape, BF),
             pltpu.VMEM((n_dim, n_fact, block, block), F32),
-            pltpu.SemaphoreType.DMA((5,)),
+            pltpu.SemaphoreType.DMA((4,)),
         ],
         compiler_params=pltpu.CompilerParams(vmem_limit_bytes=small),
         name="prep",
-    )(links.T, link_count, block_table, tiles, w_tables)
+    )(stay(links.T), link_count, stay(block_table), stay(tiles), stay(w_tables))
 
     def sems(*shape):
-        return [pltpu.SemaphoreType.DMA((STAGES, *shape))] * 2
+        return pltpu.SemaphoreType.DMA(shape)
 
     held = STAGES // CORES
     fact_out, grad_dims, weights = pl.pallas_call(
@@ -477,14 +465,9 @@
             pltpu.VMEM((held, (tables + 1) * depth, cut), F32),
             pltpu.VMEM((held, n_fact, part, cut), BF),
             pltpu.VMEM((held, n_fact, part, cut), BF),
-            *sems(n_fact),
-            *[pltpu.SemaphoreType.DMA((n_dim,))] * 2,
-            *sems(chips), *sems(chips), *sems(chips), *sems(chips),
-            *sems(n_fact),
-            pltpu.SemaphoreType.DMA((STAGES, chips)),
-            pltpu.SemaphoreType.DMA((STAGES, chips, CORES)),
-            *sems(n_fact), *sems(n_fact),
-            *sems(n_fact, chips), *sems(n_fact, chips),
+            sems(12), sems(STAGES), sems(1),
+            *[sems(STAGES)] * 7,
+            sems(STAGES, n_fact), sems(STAGES, n_fact), sems(STAGES),
         ],
         compiler_params=pltpu.CompilerParams(
             collective_id=0, has_side_effects=True, vmem_limit_bytes=grant

time: 72.8 us -> 65.1 us (0.89)
  Pallas kernels: 67.7 us -> 63.2 us
  local copies, waits for them, and re-layouts: 3.98 us -> 0.02 us
    pallas_call x1, Pallas kernels: 64.2 us -> 59.2 us  [body(): pl.pallas_call(functools.partial(main_kernel, dims_n), out_shape=(jax.Sha...]
    unnamed x18 -> x10, local copies, waits for them, and re-layouts: 3.98 us -> 0.02 us
where the time goes in v2:
time: 65.1 us; the launch traced here: 64.7 us
  Pallas kernels  63.2 us (97%)
  between operations  1.45 us (2%)
    pallas_call x1, Pallas kernels, body(): pl.pallas_call(functools.partial(main_kernel, dims_n), out_shape=(jax.Sha...  59.2 us
    pallas_call x1, Pallas kernels, body(): pl.pallas_call(post_kernel, out_shape=(jax.ShapeDtypeStruct((rows, width)...  2.2 us
    pallas_call x1, Pallas kernels, body(): pl.pallas_call(functools.partial(prep_kernel, dims_n), out_shape=(jax.Sha...  1.82 us

profile of v2, /device:TPU:0, one launch (start us, length us, event | category | flops | bytes accessed | tf_op | source)
XLA Modules:
  0.0 64.7 jit_solution(16289989775965193553)
XLA Ops:
  0.6 0.0 copy-start.4
  0.6 0.0 copy-start.3
  0.7 0.0 copy-start
  0.7 0.0 copy-start.2
  0.7 0.0 copy-start.1
  1.4 1.8 %prep.1 = (bf16[1024,512]{1,0:T(8,128)(2,1)S(1)}, bf16[512,512]{1,0:T(8,128)(2,1)S(1)}) custom-call(s32[2,32]{1,0:T(2,128)} %bitcast.1, s32[1]{0:T(128)S(6)} %copy.13.count, s32[32]{0:T(128)} %table.1, bf16[32,128,128]{2,1,0:T(8,128)(2,1)} %tiles_h.1, bf16[3,512,512]{2,1,0:T(8,128)(2,1)} %w_tables_h.1), custom_call_target="tpu_custom_call" | custom-call | tf_op jit(solution)/shard_map/prep/pallas_call | solution.py:414
  3.2 0.0 copy-done.4
  3.2 0.0 copy-done.3
  3.3 0.0 copy-done
  3.3 0.0 copy-done.2
  3.3 0.0 copy-done.1
  3.3 59.2 %main.1 = (bf16[128,512]{1,0:T(8,128)(2,1)S(1)}, f32[128,512]{1,0:T(8,128)S(1)}, bf16[4,4,512,128]{3,2,1,0:T(8,128)(2,1)S(1)}) custom-call(s32[32]{0:T(128)S(1)} %copy-done.4, bf16[1024,512]{1,0:T(8,128)(2,1)S(1)} %get-tuple-element.9.adj, bf16[512,512]{1,0:T(8,128)(2,1)S(1)} %get-tuple-element.10.w_one, bf16[128,512]{1,0:T(8,128)(2,1)S(1)} %copy-done.1, ...), custom_call_target="tpu_custom_call" | custom-call | tf_op jit(solution)/shard_map/main/pallas_call | solution.py:437
  62.5 2.2 %post.1 = (bf16[128,512]{1,0:T(8,128)(2,1)}, f32[128,512]{1,0:T(8,128)}, f32[512,512]{1,0:T(8,128)}, f32[3,512,512]{2,1,0:T(8,128)}) custom-call(bf16[128,512]{1,0:T(8,128)(2,1)S(1)} %get-tuple-element.11.out_in, f32[128,512]{1,0:T(8,128)S(1)} %get-tuple-element.12.dims_in, bf16[4,4,512,128]{3,2,1,0:T(8,128)(2,1)S(1)} %get-tuple-element.13.weights), custom_call_target="tpu_custom_call" | custom-call | tf_op jit(solution)/shard_map/post/pallas_call | solution.py:477
Async XLA Ops:
  0.6 2.6 %copy-start.4 = (s32[32]{0:T(128)S(1)}, s32[32]{0:T(128)}, u32[]{:S(2)}) copy-start(s32[32]{0:T(128)} %table.1) | copy-start | bytes 388
  0.6 2.6 %copy-start.3 = (bf16[128,512]{1,0:T(8,128)(2,1)S(1)}, bf16[128,512]{1,0:T(8,128)(2,1)}, u32[]{:S(2)}) copy-start(bf16[128,512]{1,0:T(8,128)(2,1)} %cot.1) | copy-start | bytes 393220
  0.7 2.6 %copy-start = (bf16[512,512]{1,0:T(8,128)(2,1)S(1)}, bf16[512,512]{1,0:T(8,128)(2,1)}, u32[]{:S(2)}) copy-start(bf16[512,512]{1,0:T(8,128)(2,1)} %w_self.1) | copy-start | bytes 1572868
  0.7 2.6 %copy-start.2 = (bf16[128,512]{1,0:T(8,128)(2,1)S(1)}, bf16[128,512]{1,0:T(8,128)(2,1)}, u32[]{:S(2)}) copy-start(bf16[128,512]{1,0:T(8,128)(2,1)} %dims.1) | copy-start | bytes 393220
  0.7 2.6 %copy-start.1 = (bf16[128,512]{1,0:T(8,128)(2,1)S(1)}, bf16[128,512]{1,0:T(8,128)(2,1)}, u32[]{:S(2)}) copy-start(bf16[128,512]{1,0:T(8,128)(2,1)} %facts.1) | copy-start | bytes 393220

commit v3 on v2

--- a/solution.py
+++ b/solution.py
@@ -22,7 +22,7 @@
     return x.astype(F32).T.astype(BF)
 
 
-def prep_kernel(dims_n, links_h, count, table_h, tiles_h, w_tables_h, adj, w_one, links, table, tiles, acc, sems):
+def prep_kernel(dims_n, links_h, count, table_h, tiles_h, w_tables_h, adj, w_one, names, links, table, tiles, acc, sems):
     n_fact, n_dim = dims_n
     chips = n_dim // CORES
     block = tiles.shape[1]
@@ -41,6 +41,10 @@
     own = table[f * n_dim + d]
     weight = pltpu.make_async_copy(w_tables_h.at[own], w_one, sems.at[3])
     weight.start()
+    for i in range(n_dim):
+        source = (i % chips) * CORES + i // chips
+        name = table[f * n_dim + source].astype(F32)
+        names[i : i + 1, :] = jnp.full((1, names.shape[1]), name, F32)
     small[1].wait()
     load.wait()
 
@@ -59,7 +63,7 @@
 
 
 def main_kernel(
-    dims_n, table, adj, w_one, facts, dims, cot, w_self,
+    dims_n, names, adj, w_one, facts, dims, cot, w_self,
     fact_out, grad_dims, weights,
     proj, chunks, panel, adj_t, chunk_all, masked, pre, send1, recv1, mine, send2, recv2, gp, grad,
     send3, recv3, gs, gs_all, w_own, w_send, w_recv,
@@ -247,8 +251,7 @@
     def mask():
         arrive(chunk_all.at[:, pl.ds(rows, (n_dim - 1) * rows)], f_r.at[0])
         for i in range(n_dim):
-            source = (i % chips) * CORES + i // chips
-            name = table[f * n_dim + source]
+            name = names[i : i + 1, :]
             lanes = slice(i * rows, (i + 1) * rows)
             values = chunk_all[depth:, lanes].astype(F32)
             for t in range(tables):
@@ -336,11 +339,11 @@
                     copy_q(h, i, j).start()
 
     tasks = [
-        (0.0, forward), (1.5, pair), (5.2, activate), (8.8, share), (9.9, backward),
-        (15.4, collect), (19.1, table_weight), (23.4, finish), (27.4, relay), (32.0, hand),
+        (0.0, 3.2, forward), (1.5, 3.2, pair), (6.4, 3.2, activate), (10.0, 3.2, share),
+        (11.1, 3.7, backward), (16.6, 3.7, collect), (20.3, 3.7, table_weight),
+        (24.6, 3.7, finish), (28.6, 3.7, relay), (33.2, 3.7, hand),
     ]
-    step = 2.5
-    plan = [(at + step * h, h, task) for at, task in tasks for h in every]
+    plan = [(at + step * h, h, task) for at, step, task in tasks for h in every]
     plan.append((6.0, 0, lambda h: mask()))
     for _, h, task in sorted(plan, key=lambda item: item[:2]):
         task(h)
@@ -377,13 +380,12 @@
     for copy in started:
         copy.start()
     for t in range(tables):
+        target = w_tables.at[t - 1] if t else w_self
         for h in range(stages):
-            wide[t, :, h * cut : (h + 1) * cut] = weights[h, t].astype(F32)
-        copy = pltpu.make_async_copy(
-            wide.at[t], w_tables.at[t - 1] if t else w_self, sems.at[t]
-        )
-        copy.start()
-        started.append(copy)
+            lanes = pl.ds(h * cut, cut)
+            wide[t, :, lanes] = weights[h, t].astype(F32)
+            pltpu.make_async_copy(wide.at[t, :, lanes], target.at[:, lanes], sems.at[t]).start()
+        started.append(pltpu.make_async_copy(wide.at[t], target, sems.at[t]))
     for copy in started:
         copy.wait()
 
@@ -411,14 +413,15 @@
     def stay(x):
         return pltpu.with_memory_space_constraint(x, pltpu.HBM)
 
-    adj, w_one = pl.pallas_call(
+    adj, w_one, names = pl.pallas_call(
         functools.partial(prep_kernel, dims_n),
         out_shape=(
             jax.ShapeDtypeStruct((n_dim * rows, n_fact * rows), BF),
             jax.ShapeDtypeStruct((width, width), BF),
+            jax.ShapeDtypeStruct((n_dim, rows), F32),
         ),
         in_specs=[hbm, smem, hbm, hbm, hbm],
-        out_specs=(vmem, vmem),
+        out_specs=(vmem, vmem, vmem),
         scratch_shapes=[
             pltpu.SMEM(links.shape[::-1], jnp.int32),
             pltpu.SMEM(block_table.shape, jnp.int32),
@@ -441,7 +444,7 @@
             jax.ShapeDtypeStruct((rows, width), F32),
             jax.ShapeDtypeStruct((STAGES, tables + 1, width, cut), BF),
         ),
-        in_specs=[smem] + [vmem] * 6,
+        in_specs=[vmem] * 7,
         out_specs=(vmem, vmem, vmem),
         scratch_shapes=[
             pltpu.VMEM((STAGES, rows, cut), BF),
@@ -473,7 +476,7 @@
             collective_id=0, has_side_effects=True, vmem_limit_bytes=grant
         ),
         name="main",
-    )(block_table, adj, w_one, facts, dims, cot, w_self)
+    )(names, adj, w_one, facts, dims, cot, w_self)
     return pl.pallas_call(
         post_kernel,
         out_shape=(

time: 65.1 us -> 63.2 us (0.971)
  Pallas kernels: 63.2 us -> 61.8 us
    pallas_call x1, Pallas kernels: 59.2 us -> 57.8 us  [body(): pl.pallas_call(functools.partial(main_kernel, dims_n), out_shape=(jax.Sha...]
where the time goes in v3:
time: 63.2 us; the launch traced here: 63.3 us
  Pallas kernels  61.8 us (98%)
  between operations  1.44 us (2%)
    pallas_call x1, Pallas kernels, body(): pl.pallas_call(functools.partial(main_kernel, dims_n), out_shape=(jax.Sha...  57.8 us
    pallas_call x1, Pallas kernels, body(): pl.pallas_call(post_kernel, out_shape=(jax.ShapeDtypeStruct((rows, width)...  2.17 us
    pallas_call x1, Pallas kernels, body(): pl.pallas_call(functools.partial(prep_kernel, dims_n), out_shape=(jax.Sha...  1.82 us

profile of v3, /device:TPU:0, one launch (start us, length us, event | category | flops | bytes accessed | tf_op | source)
XLA Modules:
  0.0 63.3 jit_solution(9055781195084876279)
XLA Ops:
  0.6 0.0 copy-start.3
  0.6 0.0 copy-start
  0.7 0.0 copy-start.2
  0.7 0.0 copy-start.1
  1.4 1.8 %prep.1 = (bf16[1024,512]{1,0:T(8,128)(2,1)S(1)}, bf16[512,512]{1,0:T(8,128)(2,1)S(1)}, f32[8,128]{1,0:T(8,128)S(1)}) custom-call(s32[2,32]{1,0:T(2,128)} %bitcast.1, s32[1]{0:T(128)S(6)} %copy.13.count, s32[32]{0:T(128)} %table_h.1, bf16[32,128,128]{2,1,0:T(8,128)(2,1)} %tiles_h.1, bf16[3,512,512]{2,1,0:T(8,128)(2,1)} %w_tables_h.1), custom_call_target="tpu_custom_call" | custom-call | tf_op jit(solution)/shard_map/prep/pallas_call | solution.py:416
  3.2 0.0 copy-done.3
  3.2 0.0 copy-done
  3.2 0.0 copy-done.2
  3.3 0.0 copy-done.1
  3.3 57.8 %main.1 = (bf16[128,512]{1,0:T(8,128)(2,1)S(1)}, f32[128,512]{1,0:T(8,128)S(1)}, bf16[4,4,512,128]{3,2,1,0:T(8,128)(2,1)S(1)}) custom-call(f32[8,128]{1,0:T(8,128)S(1)} %get-tuple-element.10.names, bf16[1024,512]{1,0:T(8,128)(2,1)S(1)} %get-tuple-element.11.adj, bf16[512,512]{1,0:T(8,128)(2,1)S(1)} %get-tuple-element.12.w_one, ...), custom_call_target="tpu_custom_call" | custom-call | tf_op jit(solution)/shard_map/main/pallas_call | solution.py:440
  61.1 2.2 %post.1 = (bf16[128,512]{1,0:T(8,128)(2,1)}, f32[128,512]{1,0:T(8,128)}, f32[512,512]{1,0:T(8,128)}, f32[3,512,512]{2,1,0:T(8,128)}) custom-call(bf16[128,512]{1,0:T(8,128)(2,1)S(1)} %get-tuple-element.13.out_in, f32[128,512]{1,0:T(8,128)S(1)} %get-tuple-element.14.dims_in, bf16[4,4,512,128]{3,2,1,0:T(8,128)(2,1)S(1)} %get-tuple-element.15.weights), custom_call_target="tpu_custom_call" | custom-call | tf_op jit(solution)/shard_map/post/pallas_call | solution.py:480
Async XLA Ops:
  0.6 2.6 %copy-start.3 = (bf16[128,512]{1,0:T(8,128)(2,1)S(1)}, bf16[128,512]{1,0:T(8,128)(2,1)}, u32[]{:S(2)}) copy-start(bf16[128,512]{1,0:T(8,128)(2,1)} %cot.1) | copy-start | bytes 393220
  0.6 2.6 %copy-start = (bf16[512,512]{1,0:T(8,128)(2,1)S(1)}, bf16[512,512]{1,0:T(8,128)(2,1)}, u32[]{:S(2)}) copy-start(bf16[512,512]{1,0:T(8,128)(2,1)} %w_self.1) | copy-start | bytes 1572868
  0.7 2.6 %copy-start.2 = (bf16[128,512]{1,0:T(8,128)(2,1)S(1)}, bf16[128,512]{1,0:T(8,128)(2,1)}, u32[]{:S(2)}) copy-start(bf16[128,512]{1,0:T(8,128)(2,1)} %dims.1) | copy-start | bytes 393220
  0.7 2.6 %copy-start.1 = (bf16[128,512]{1,0:T(8,128)(2,1)S(1)}, bf16[128,512]{1,0:T(8,128)(2,1)}, u32[]{:S(2)}) copy-start(bf16[128,512]{1,0:T(8,128)(2,1)} %facts.1) | copy-start | bytes 393220
